TPU v7x, 1024 devices: a whole 8x8x8 slice. The times are simulated.
1024 devices in a mesh: gx: 16 (over z, core), gy: 64 (over x, y).
Axes of the slice: x: 8, y: 8, z: 8, core: 2. Of those that a mesh axis runs over, the one named last changes fastest.
Arguments:
- flow_populations: float32 [19, 256, 512, 128], P(None, 'gx', 'gy'), may hold values from 0 to 1, as said below
- solute_populations: float32 [7, 256, 512, 128], P(None, 'gx', 'gy'), may hold values from 0 to 1, as said below
- voxel_kind: int32 [256, 512, 128], P('gx', 'gy'), may hold values from 0 to 3, as said below
Outputs:
- density: float32 [256, 512, 128], P('gx', 'gy')
- momentum: float32 [3, 256, 512, 128], P(None, 'gx', 'gy')
- concentration: float32 [256, 512, 128], P('gx', 'gy')
Inputs may be any that keep to these rules, and one draw needn't show every extreme that they name: `flow_populations`: each flow population is its lattice weight w_i times a factor between 0.5 and 1.5. `solute_populations`: each solute population is its lattice weight v_k times a positive factor of at most 1.9. `voxel_kind`: the first z plane holds only inlet and solid voxels, the last z plane only outlet and solid voxels, every other plane only pore and solid voxels.
All inputs are finite; a program needn't handle non-finite values.
Results may differ from a plain program's by a relative error of at most 0.0001.
Values sent between devices are 32-bit elements; how exact they have to be, the bound alone decides.
A program may use at most 32 MiB of HBM per device.

v0:
```python
import jax
import jax.numpy as jnp
from jax import lax
from jax.sharding import PartitionSpec as P

STEPS = 3


flow_velocity = [
    (0, 0, 0),
    (1, 0, 0),
    (-1, 0, 0),
    (0, 1, 0),
    (0, -1, 0),
    (0, 0, 1),
    (0, 0, -1),
    (1, 1, 0),
    (-1, -1, 0),
    (1, -1, 0),
    (-1, 1, 0),
    (1, 0, 1),
    (-1, 0, -1),
    (1, 0, -1),
    (-1, 0, 1),
    (0, 1, 1),
    (0, -1, -1),
    (0, 1, -1),
    (0, -1, 1),
]
flow_weight = [1.0 / 3.0] + [1.0 / 18.0] * 6 + [1.0 / 36.0] * 12
solute_velocity = flow_velocity[:7]
solute_weight = [0.25] + [0.125] * 6
all_velocity = flow_velocity + solute_velocity
flow_plus = 1.25
flow_minus = 1.0 / 1.125
solute_plus = 1.0 / 1.75
solute_minus = 1.0 / 0.7
inlet_density = 1.05
outlet_density = 0.95
inlet_solute = 1.0


def padded_2(block, sides, width):
    for axis, dim in sides:
        count = lax.axis_size(axis)
        forward = [(i, i + 1) for i in range(count - 1)]
        forward.append((count - 1, 0))
        backward = [(target, source) for source, target in forward]
        low = lax.ppermute(
            lax.slice_in_dim(block, block.shape[dim] - width, None, axis=dim), axis, forward
        )
        high = lax.ppermute(lax.slice_in_dim(block, 0, width, axis=dim), axis, backward)
        block = jnp.concatenate([low, block, high], axis=dim)
    return block


def opposite(component):
    if component == 0:
        return 0
    if component % 2 == 1:
        return component + 1
    return component - 1


def moments(flow):
    density = jnp.sum(flow, axis=0)
    components = []
    for axis_number in range(3):
        summed = jnp.zeros_like(density)
        for component, velocity in enumerate(flow_velocity):
            if velocity[axis_number] != 0:
                summed = summed + velocity[axis_number] * flow[component]
        components.append(summed)
    return (density, components)


def collide(flow, solute, voxel_kind):
    density, (mom_x, mom_y, mom_z) = moments(flow)
    concentration = jnp.sum(solute, axis=0)
    square = mom_x * mom_x + mom_y * mom_y + mom_z * mom_z
    is_fluid = voxel_kind == 0
    is_inlet = voxel_kind == 2
    is_outlet = voxel_kind == 3
    outgoing = []
    for component, velocity in enumerate(flow_velocity):
        weight = flow_weight[component]
        mirror = opposite(component)
        projection = velocity[0] * mom_x + velocity[1] * mom_y + velocity[2] * mom_z
        even_eq = weight * (density + 4.5 * projection * projection - 1.5 * square)
        odd_eq = weight * 3.0 * projection
        even_part = 0.5 * (flow[component] + flow[mirror])
        odd_part = 0.5 * (flow[component] - flow[mirror])
        relaxed = (
            flow[component] - flow_plus * (even_part - even_eq) - flow_minus * (odd_part - odd_eq)
        )
        result = jnp.where(is_fluid, relaxed, flow[mirror])
        result = jnp.where(is_inlet, weight * inlet_density, result)
        result = jnp.where(is_outlet, weight * outlet_density, result)
        outgoing.append(result)
    for component, velocity in enumerate(solute_velocity):
        weight = solute_weight[component]
        mirror = opposite(component)
        projection = velocity[0] * mom_x + velocity[1] * mom_y + velocity[2] * mom_z
        even_eq = weight * concentration
        odd_eq = weight * 4.0 * concentration * projection
        even_part = 0.5 * (solute[component] + solute[mirror])
        odd_part = 0.5 * (solute[component] - solute[mirror])
        relaxed = (
            solute[component]
            - solute_plus * (even_part - even_eq)
            - solute_minus * (odd_part - odd_eq)
        )
        result = jnp.where(is_fluid, relaxed, solute[mirror])
        result = jnp.where(is_inlet, weight * inlet_solute, result)
        result = jnp.where(is_outlet, jnp.zeros_like(result), result)
        outgoing.append(result)
    return jnp.stack(outgoing)


def depth_shift(section, along_z):
    if along_z == 1:
        return jnp.concatenate([jnp.zeros_like(section[:, :, :1]), section[:, :, :-1]], axis=2)
    if along_z == -1:
        return jnp.concatenate([section[:, :, 1:], jnp.zeros_like(section[:, :, :1])], axis=2)
    return section


def propagate(stacked):
    cells_x = stacked.shape[1]
    cells_y = stacked.shape[2]
    planes = []
    padded = padded_2(stacked, (("gx", 1), ("gy", 2)), 1)
    for component, velocity in enumerate(all_velocity):
        section = padded[
            component,
            1 - velocity[0] : 1 - velocity[0] + cells_x,
            1 - velocity[1] : 1 - velocity[1] + cells_y,
            :,
        ]
        planes.append(depth_shift(section, velocity[2]))
    return jnp.stack(planes)


def local(flow_populations, solute_populations, voxel_kind):
    flow = flow_populations
    solute = solute_populations
    for sweep in range(STEPS):
        outgoing = collide(flow, solute, voxel_kind)
        shifted = propagate(outgoing)
        flow = shifted[:19]
        solute = shifted[19:]
    density, components = moments(flow)
    return (density, jnp.stack(components), jnp.sum(solute, axis=0))


def solution(mesh):
    placed = (P(None, "gx", "gy", None), P(None, "gx", "gy", None), P("gx", "gy", None))
    return jax.shard_map(
        local,
        mesh=mesh,
        in_specs=placed,
        out_specs=(P("gx", "gy", None), P(None, "gx", "gy", None), P("gx", "gy", None)),
        check_vma=False,
    )
```

profile of v0, /device:TPU:8, one launch (start us, length us, event | category | flops | bytes accessed | tf_op | source)
XLA Modules:
  0.0 91.7 jit_solution(13230036984732306779)
XLA Ops:
  0.6 1.5 %reduce_sum.330 = f32[16,8,128]{2,1,0:T(8,128)S(1)} reduce(f32[19,16,8,128]{3,2,1,0:T(8,128)} %param.3, f32[]{:T(128)} %constant.2.clone.1), dimensions={0}, to_apply=%region_0.0 | reduce | flops 294912 | bytes 1310724 | tf_op jit(solution)/shard_map/reduce_sum | solution.py:66
  2.1 1.1 %reduce_sum.331 = f32[16,8,128]{2,1,0:T(8,128)S(1)} reduce(f32[7,16,8,128]{3,2,1,0:T(8,128)} %param.4, f32[]{:T(128)} %constant.2.clone.1), dimensions={0}, to_apply=%region_1.0 | reduce | flops 98304 | bytes 524292 | tf_op jit(solution)/shard_map/reduce_sum | solution.py:79
  3.2 0.2 constant_dynamic-update-slice_fusion.25
  4.8 0.5 copy-done.1
  5.8 14.9 %collective-permute-start.1 = (f32[26,1,8,128]{3,2,1,0:T(8,128)S(1)}, f32[26,1,8,128]{3,2,1,0:T(8,128)S(1)}, u32[]{:S(2)}, u32[]{:S(2)}) collective-permute-start(f32[26,1,8,128]{3,2,1,0:T(8,128)S(1)} %get-tuple-element.160), channel_id=1, source_target_pairs={{64,0},{128,64},{192,128},{256,192},{320,256},{384,320},{448,384},... | collective-permute-start | bytes 319496 | tf_op jit(solution)/shard_map/ppermute | solution.py:52
  20.6 2.4 %collective-permute-done = f32[26,1,8,128]{3,2,1,0:T(8,128)S(1)} collective-permute-done((f32[26,1,8,128]{3,2,1,0:T(8,128)S(1)}, f32[26,1,8,128]{3,2,1,0:T(8,128)S(1)}, u32[]{:S(2)}, u32[]{:S(2)}) %collective-permute-start) | collective-permute-done | bytes 106528 | tf_op jit(solution)/shard_map/ppermute | solution.py:49
  23.0 0.3 pad_maximum_fusion.8
  23.3 3.6 %collective-permute-start.2 = (f32[26,18,1,128]{3,2,1,0:T(1,128)S(1)}, f32[26,18,1,128]{3,2,1,0:T(1,128)S(1)}, u32[]{:S(2)}, u32[]{:S(2)}) collective-permute-start(f32[26,18,1,128]{3,2,1,0:T(1,128)S(1)} %get-tuple-element.141), channel_id=1, source_target_pairs={{0,1},{1,2},{2,3},{3,4},{4,5},{5,6},{6,7},{7,8},{8,9},{9,10},{10,1... | collective-permute-start | bytes 718856 | tf_op jit(solution)/shard_map/ppermute | solution.py:49
  26.9 5.6 %collective-permute-start.3 = (f32[26,18,1,128]{3,2,1,0:T(1,128)S(1)}, f32[26,18,1,128]{3,2,1,0:T(1,128)S(1)}, u32[]{:S(2)}, u32[]{:S(2)}) collective-permute-start(f32[26,18,1,128]{3,2,1,0:T(1,128)S(1)} %get-tuple-element.142), channel_id=1, source_target_pairs={{1,0},{2,1},{3,2},{4,3},{5,4},{6,5},{7,6},{8,7},{9,8},{10,9},{11,1... | collective-permute-start | bytes 718856 | tf_op jit(solution)/shard_map/ppermute | solution.py:52
  32.7 1.9 %collective-permute-done.2 = f32[26,18,1,128]{3,2,1,0:T(1,128)S(1)} collective-permute-done((f32[26,18,1,128]{3,2,1,0:T(1,128)S(1)}, f32[26,18,1,128]{3,2,1,0:T(1,128)S(1)}, u32[]{:S(2)}, u32[]{:S(2)}) %collective-permute-start.2) | collective-permute-done | bytes 239648 | tf_op jit(solution)/shard_map/ppermute | solution.py:49
  34.6 1.5 %collective-permute-done.3 = f32[26,18,1,128]{3,2,1,0:T(1,128)S(1)} collective-permute-done((f32[26,18,1,128]{3,2,1,0:T(1,128)S(1)}, f32[26,18,1,128]{3,2,1,0:T(1,128)S(1)}, u32[]{:S(2)}, u32[]{:S(2)}) %collective-permute-start.3) | collective-permute-done | bytes 239648 | tf_op jit(solution)/shard_map/ppermute | solution.py:52
  36.4 0.3 constant_dynamic-update-slice_fusion.51
  37.2 0.1 constant_dynamic-update-slice_fusion.45
  37.7 0.1 constant_dynamic-update-slice_fusion.39
  37.9 0.1 constant_dynamic-update-slice_fusion.38
  38.2 0.1 constant_dynamic-update-slice_fusion.35
  38.4 0.1 constant_dynamic-update-slice_fusion.34
  38.6 0.1 constant_dynamic-update-slice_fusion.32
  39.0 0.1 constant_dynamic-update-slice_fusion.27
  39.1 0.1 constant_dynamic-update-slice_fusion.26
  39.3 4.2 %collective-permute-start.5 = (f32[26,1,8,128]{3,2,1,0:T(8,128)S(1)}, f32[26,1,8,128]{3,2,1,0:T(8,128)S(1)}, u32[]{:S(2)}, u32[]{:S(2)}) collective-permute-start(f32[26,1,8,128]{3,2,1,0:T(8,128)S(1)} %get-tuple-element.157), channel_id=1, source_target_pairs={{64,0},{128,64},{192,128},{256,192},{320,256},{384,320},{448,384},... | collective-permute-start | bytes 319496 | tf_op jit(solution)/shard_map/ppermute | solution.py:52
  43.5 2.4 %collective-permute-done.4 = f32[26,1,8,128]{3,2,1,0:T(8,128)S(1)} collective-permute-done((f32[26,1,8,128]{3,2,1,0:T(8,128)S(1)}, f32[26,1,8,128]{3,2,1,0:T(8,128)S(1)}, u32[]{:S(2)}, u32[]{:S(2)}) %collective-permute-start.4) | collective-permute-done | bytes 106528 | tf_op jit(solution)/shard_map/ppermute | solution.py:49
  45.9 0.3 pad_maximum_fusion.5
  46.2 2.4 %collective-permute-start.6 = (f32[26,18,1,128]{3,2,1,0:T(1,128)S(1)}, f32[26,18,1,128]{3,2,1,0:T(1,128)S(1)}, u32[]{:S(2)}, u32[]{:S(2)}) collective-permute-start(f32[26,18,1,128]{3,2,1,0:T(1,128)S(1)} %get-tuple-element.137), channel_id=1, source_target_pairs={{0,1},{1,2},{2,3},{3,4},{4,5},{5,6},{6,7},{7,8},{8,9},{9,10},{10,1... | collective-permute-start | bytes 718856 | tf_op jit(solution)/shard_map/ppermute | solution.py:49
  48.6 7.2 %collective-permute-start.7 = (f32[26,18,1,128]{3,2,1,0:T(1,128)S(1)}, f32[26,18,1,128]{3,2,1,0:T(1,128)S(1)}, u32[]{:S(2)}, u32[]{:S(2)}) collective-permute-start(f32[26,18,1,128]{3,2,1,0:T(1,128)S(1)} %get-tuple-element.138), channel_id=1, source_target_pairs={{1,0},{2,1},{3,2},{4,3},{5,4},{6,5},{7,6},{8,7},{9,8},{10,9},{11,1... | collective-permute-start | bytes 718856 | tf_op jit(solution)/shard_map/ppermute | solution.py:52
  56.1 1.9 %collective-permute-done.6 = f32[26,18,1,128]{3,2,1,0:T(1,128)S(1)} collective-permute-done((f32[26,18,1,128]{3,2,1,0:T(1,128)S(1)}, f32[26,18,1,128]{3,2,1,0:T(1,128)S(1)}, u32[]{:S(2)}, u32[]{:S(2)}) %collective-permute-start.6) | collective-permute-done | bytes 239648 | tf_op jit(solution)/shard_map/ppermute | solution.py:49
  58.0 1.5 %collective-permute-done.7 = f32[26,18,1,128]{3,2,1,0:T(1,128)S(1)} collective-permute-done((f32[26,18,1,128]{3,2,1,0:T(1,128)S(1)}, f32[26,18,1,128]{3,2,1,0:T(1,128)S(1)}, u32[]{:S(2)}, u32[]{:S(2)}) %collective-permute-start.7) | collective-permute-done | bytes 239648 | tf_op jit(solution)/shard_map/ppermute | solution.py:52
  59.8 0.3 constant_dynamic-update-slice_fusion.77
  60.6 0.1 constant_dynamic-update-slice_fusion.71
  61.1 0.1 constant_dynamic-update-slice_fusion.65
  61.3 0.1 constant_dynamic-update-slice_fusion.64
  61.6 0.1 constant_dynamic-update-slice_fusion.61
  61.8 0.1 constant_dynamic-update-slice_fusion.60
  62.0 0.1 constant_dynamic-update-slice_fusion.58
  62.4 0.1 constant_dynamic-update-slice_fusion.53
  62.5 0.1 constant_dynamic-update-slice_fusion.52
  62.7 4.5 %collective-permute-start.9 = (f32[26,1,8,128]{3,2,1,0:T(8,128)S(1)}, f32[26,1,8,128]{3,2,1,0:T(8,128)S(1)}, u32[]{:S(2)}, u32[]{:S(2)}) collective-permute-start(f32[26,1,8,128]{3,2,1,0:T(8,128)S(1)} %get-tuple-element.154), channel_id=1, source_target_pairs={{64,0},{128,64},{192,128},{256,192},{320,256},{384,320},{448,384},... | collective-permute-start | bytes 319496 | tf_op jit(solution)/shard_map/ppermute | solution.py:52
  67.2 2.4 %collective-permute-done.8 = f32[26,1,8,128]{3,2,1,0:T(8,128)S(1)} collective-permute-done((f32[26,1,8,128]{3,2,1,0:T(8,128)S(1)}, f32[26,1,8,128]{3,2,1,0:T(8,128)S(1)}, u32[]{:S(2)}, u32[]{:S(2)}) %collective-permute-start.8) | collective-permute-done | bytes 106528 | tf_op jit(solution)/shard_map/ppermute | solution.py:49
  69.6 0.3 pad_maximum_fusion
  69.9 7.5 %collective-permute-start.11 = (f32[26,18,1,128]{3,2,1,0:T(1,128)S(1)}, f32[26,18,1,128]{3,2,1,0:T(1,128)S(1)}, u32[]{:S(2)}, u32[]{:S(2)}) collective-permute-start(f32[26,18,1,128]{3,2,1,0:T(1,128)S(1)} %get-tuple-element.133), channel_id=1, source_target_pairs={{1,0},{2,1},{3,2},{4,3},{5,4},{6,5},{7,6},{8,7},{9,8},{10,9},{11,1... | collective-permute-start | bytes 718856 | tf_op jit(solution)/shard_map/ppermute | solution.py:52
  77.4 1.9 %collective-permute-start.10 = (f32[26,18,1,128]{3,2,1,0:T(1,128)S(1)}, f32[26,18,1,128]{3,2,1,0:T(1,128)S(1)}, u32[]{:S(2)}, u32[]{:S(2)}) collective-permute-start(f32[26,18,1,128]{3,2,1,0:T(1,128)S(1)} %get-tuple-element.134), channel_id=1, source_target_pairs={{0,1},{1,2},{2,3},{3,4},{4,5},{5,6},{6,7},{7,8},{8,9},{9,10},{10,1... | collective-permute-start | bytes 718856 | tf_op jit(solution)/shard_map/ppermute | solution.py:49
  79.6 1.4 %collective-permute-done.11 = f32[26,18,1,128]{3,2,1,0:T(1,128)S(1)} collective-permute-done((f32[26,18,1,128]{3,2,1,0:T(1,128)S(1)}, f32[26,18,1,128]{3,2,1,0:T(1,128)S(1)}, u32[]{:S(2)}, u32[]{:S(2)}) %collective-permute-start.11) | collective-permute-done | bytes 239648 | tf_op jit(solution)/shard_map/ppermute | solution.py:52
  81.0 7.7 %collective-permute-done.10 = f32[26,18,1,128]{3,2,1,0:T(1,128)S(1)} collective-permute-done((f32[26,18,1,128]{3,2,1,0:T(1,128)S(1)}, f32[26,18,1,128]{3,2,1,0:T(1,128)S(1)}, u32[]{:S(2)}, u32[]{:S(2)}) %collective-permute-start.10) | collective-permute-done | bytes 239648 | tf_op jit(solution)/shard_map/ppermute | solution.py:49
  89.0 0.2 add_bitcast_fusion
  89.2 0.1 add_bitcast_fusion.2
  89.5 0.7 pad_maximum_fusion.9
  90.2 0.8 add_add_fusion
  90.9 0.7 fusion.621
  (98 shorter events, 6.5 us)
Async XLA Ops:
  0.6 2.5 %copy-start = (f32[19,16,8,128]{3,2,1,0:T(8,128)S(1)}, f32[19,16,8,128]{3,2,1,0:T(8,128)}, u32[]{:S(2)}) copy-start(f32[19,16,8,128]{3,2,1,0:T(8,128)} %param.3) | copy-start | bytes 3735556
  0.6 2.5 %copy-start.2 = (s32[16,8,128]{2,1,0:T(8,128)S(1)}, s32[16,8,128]{2,1,0:T(8,128)}, u32[]{:S(2)}) copy-start(s32[16,8,128]{2,1,0:T(8,128)} %param.5) | copy-start | bytes 196612
  4.2 1.0 %copy-start.1 = (f32[7,16,8,128]{3,2,1,0:T(8,128)S(1)}, f32[7,16,8,128]{3,2,1,0:T(8,128)}, u32[]{:S(2)}) copy-start(f32[7,16,8,128]{3,2,1,0:T(8,128)} %param.4) | copy-start | bytes 1376260
  5.7 17.2 %collective-permute-start = (f32[26,1,8,128]{3,2,1,0:T(8,128)S(1)}, f32[26,1,8,128]{3,2,1,0:T(8,128)S(1)}, u32[]{:S(2)}, u32[]{:S(2)}) collective-permute-start(f32[26,1,8,128]{3,2,1,0:T(8,128)S(1)} %get-tuple-element.159), channel_id=1, source_target_pairs={{0,64},{64,128},{128,192},{192,256},{256,320},{320,384},{384,448},... | collective-permute-start | bytes 319496 | tf_op jit(solution)/shard_map/ppermute | solution.py:49
  5.8 17.2 %collective-permute-start.1 = (f32[26,1,8,128]{3,2,1,0:T(8,128)S(1)}, f32[26,1,8,128]{3,2,1,0:T(8,128)S(1)}, u32[]{:S(2)}, u32[]{:S(2)}) collective-permute-start(f32[26,1,8,128]{3,2,1,0:T(8,128)S(1)} %get-tuple-element.160), channel_id=1, source_target_pairs={{64,0},{128,64},{192,128},{256,192},{320,256},{384,320},{448,384},... | collective-permute-start | bytes 319496 | tf_op jit(solution)/shard_map/ppermute | solution.py:52
  23.3 11.3 %collective-permute-start.2 = (f32[26,18,1,128]{3,2,1,0:T(1,128)S(1)}, f32[26,18,1,128]{3,2,1,0:T(1,128)S(1)}, u32[]{:S(2)}, u32[]{:S(2)}) collective-permute-start(f32[26,18,1,128]{3,2,1,0:T(1,128)S(1)} %get-tuple-element.141), channel_id=1, source_target_pairs={{0,1},{1,2},{2,3},{3,4},{4,5},{5,6},{6,7},{7,8},{8,9},{9,10},{10,1... | collective-permute-start | bytes 718856 | tf_op jit(solution)/shard_map/ppermute | solution.py:49
  26.9 9.2 %collective-permute-start.3 = (f32[26,18,1,128]{3,2,1,0:T(1,128)S(1)}, f32[26,18,1,128]{3,2,1,0:T(1,128)S(1)}, u32[]{:S(2)}, u32[]{:S(2)}) collective-permute-start(f32[26,18,1,128]{3,2,1,0:T(1,128)S(1)} %get-tuple-element.142), channel_id=1, source_target_pairs={{1,0},{2,1},{3,2},{4,3},{5,4},{6,5},{7,6},{8,7},{9,8},{10,9},{11,1... | collective-permute-start | bytes 718856 | tf_op jit(solution)/shard_map/ppermute | solution.py:52
  39.3 6.6 %collective-permute-start.4 = (f32[26,1,8,128]{3,2,1,0:T(8,128)S(1)}, f32[26,1,8,128]{3,2,1,0:T(8,128)S(1)}, u32[]{:S(2)}, u32[]{:S(2)}) collective-permute-start(f32[26,1,8,128]{3,2,1,0:T(8,128)S(1)} %get-tuple-element.156), channel_id=1, source_target_pairs={{0,64},{64,128},{128,192},{192,256},{256,320},{320,384},{384,448},... | collective-permute-start | bytes 319496 | tf_op jit(solution)/shard_map/ppermute | solution.py:49
  39.3 6.6 %collective-permute-start.5 = (f32[26,1,8,128]{3,2,1,0:T(8,128)S(1)}, f32[26,1,8,128]{3,2,1,0:T(8,128)S(1)}, u32[]{:S(2)}, u32[]{:S(2)}) collective-permute-start(f32[26,1,8,128]{3,2,1,0:T(8,128)S(1)} %get-tuple-element.157), channel_id=1, source_target_pairs={{64,0},{128,64},{192,128},{256,192},{320,256},{384,320},{448,384},... | collective-permute-start | bytes 319496 | tf_op jit(solution)/shard_map/ppermute | solution.py:52
  46.2 11.8 %collective-permute-start.6 = (f32[26,18,1,128]{3,2,1,0:T(1,128)S(1)}, f32[26,18,1,128]{3,2,1,0:T(1,128)S(1)}, u32[]{:S(2)}, u32[]{:S(2)}) collective-permute-start(f32[26,18,1,128]{3,2,1,0:T(1,128)S(1)} %get-tuple-element.137), channel_id=1, source_target_pairs={{0,1},{1,2},{2,3},{3,4},{4,5},{5,6},{6,7},{7,8},{8,9},{9,10},{10,1... | collective-permute-start | bytes 718856 | tf_op jit(solution)/shard_map/ppermute | solution.py:49
  48.6 10.8 %collective-permute-start.7 = (f32[26,18,1,128]{3,2,1,0:T(1,128)S(1)}, f32[26,18,1,128]{3,2,1,0:T(1,128)S(1)}, u32[]{:S(2)}, u32[]{:S(2)}) collective-permute-start(f32[26,18,1,128]{3,2,1,0:T(1,128)S(1)} %get-tuple-element.138), channel_id=1, source_target_pairs={{1,0},{2,1},{3,2},{4,3},{5,4},{6,5},{7,6},{8,7},{9,8},{10,9},{11,1... | collective-permute-start | bytes 718856 | tf_op jit(solution)/shard_map/ppermute | solution.py:52
  62.7 6.9 %collective-permute-start.8 = (f32[26,1,8,128]{3,2,1,0:T(8,128)S(1)}, f32[26,1,8,128]{3,2,1,0:T(8,128)S(1)}, u32[]{:S(2)}, u32[]{:S(2)}) collective-permute-start(f32[26,1,8,128]{3,2,1,0:T(8,128)S(1)} %get-tuple-element.153), channel_id=1, source_target_pairs={{0,64},{64,128},{128,192},{192,256},{256,320},{320,384},{384,448},... | collective-permute-start | bytes 319496 | tf_op jit(solution)/shard_map/ppermute | solution.py:49
  62.7 6.9 %collective-permute-start.9 = (f32[26,1,8,128]{3,2,1,0:T(8,128)S(1)}, f32[26,1,8,128]{3,2,1,0:T(8,128)S(1)}, u32[]{:S(2)}, u32[]{:S(2)}) collective-permute-start(f32[26,1,8,128]{3,2,1,0:T(8,128)S(1)} %get-tuple-element.154), channel_id=1, source_target_pairs={{64,0},{128,64},{192,128},{256,192},{320,256},{384,320},{448,384},... | collective-permute-start | bytes 319496 | tf_op jit(solution)/shard_map/ppermute | solution.py:52
  69.9 11.2 %collective-permute-start.11 = (f32[26,18,1,128]{3,2,1,0:T(1,128)S(1)}, f32[26,18,1,128]{3,2,1,0:T(1,128)S(1)}, u32[]{:S(2)}, u32[]{:S(2)}) collective-permute-start(f32[26,18,1,128]{3,2,1,0:T(1,128)S(1)} %get-tuple-element.133), channel_id=1, source_target_pairs={{1,0},{2,1},{3,2},{4,3},{5,4},{6,5},{7,6},{8,7},{9,8},{10,9},{11,1... | collective-permute-start | bytes 718856 | tf_op jit(solution)/shard_map/ppermute | solution.py:52
  77.4 11.3 %collective-permute-start.10 = (f32[26,18,1,128]{3,2,1,0:T(1,128)S(1)}, f32[26,18,1,128]{3,2,1,0:T(1,128)S(1)}, u32[]{:S(2)}, u32[]{:S(2)}) collective-permute-start(f32[26,18,1,128]{3,2,1,0:T(1,128)S(1)} %get-tuple-element.134), channel_id=1, source_target_pairs={{0,1},{1,2},{2,3},{3,4},{4,5},{5,6},{6,7},{7,8},{8,9},{9,10},{10,1... | collective-permute-start | bytes 718856 | tf_op jit(solution)/shard_map/ppermute | solution.py:49
where the time goes:
time: 92 us; the launch traced here: 91.7 us
  starting transfers between devices  51.9 us (56%)
  waiting for transfers between devices  23 us (25%)
  other arithmetic  13.6 us (15%)
  local copies, waits for them, and re-layouts  2 us (2%)
  between operations  1.2 us (1%)
    ppermute x6, starting transfers between devices, padded_2(): lax.ppermute(lax.slice_in_dim(block, 0, width, axis=dim), axis, backward)  43.9 us
    ppermute x6, waiting for transfers between devices, padded_2(): lax.ppermute(lax.slice_in_dim(block, block.shape[dim] - width, None, axis...  18.6 us
    ppermute x6, starting transfers between devices, padded_2(): lax.ppermute(lax.slice_in_dim(block, block.shape[dim] - width, None, axis...  8 us
    unnamed x75, other arithmetic  7.08 us
    ppermute x6, waiting for transfers between devices, padded_2(): lax.ppermute(lax.slice_in_dim(block, 0, width, axis=dim), axis, backward)  4.36 us
    reduce_sum x2, other arithmetic, moments(): density = jnp.sum(flow, axis=0)  2.26 us
  transfers between devices with their start and end apart: 12, of which 9 were waited for; matrix products, arithmetic and copies ran while one was open for 1% of the time, Pallas kernels for 0%

commit v1 on v0

v1 whole, which is shorter than its diff:
```python
import jax
import jax.numpy as jnp
from jax import lax
from jax.experimental import pallas as pl
from jax.experimental.pallas import tpu as pltpu
from jax.sharding import PartitionSpec as P

STEPS = 3
CHUNKS = 4

flow_velocity = [
    (0, 0, 0),
    (1, 0, 0),
    (-1, 0, 0),
    (0, 1, 0),
    (0, -1, 0),
    (0, 0, 1),
    (0, 0, -1),
    (1, 1, 0),
    (-1, -1, 0),
    (1, -1, 0),
    (-1, 1, 0),
    (1, 0, 1),
    (-1, 0, -1),
    (1, 0, -1),
    (-1, 0, 1),
    (0, 1, 1),
    (0, -1, -1),
    (0, 1, -1),
    (0, -1, 1),
]
flow_weight = [1.0 / 3.0] + [1.0 / 18.0] * 6 + [1.0 / 36.0] * 12
solute_velocity = flow_velocity[:7]
all_velocity = flow_velocity + solute_velocity
flow_plus = 1.25
flow_minus = 1.0 / 1.125
solute_plus = 1.0 / 1.75
solute_minus = 1.0 / 0.7
inlet_density = 1.05
outlet_density = 0.95
inlet_solute = 1.0

still = [1, 11, 13, 20, 2, 12, 14, 21, 0, 5, 6, 19, 24, 25]
upward = [7, 10, 3, 15, 17, 22]
downward = [9, 8, 4, 16, 18, 23]


def collide(f, kind):
    pore = kind == 0
    solid = kind == 1
    inlet = kind == 2
    zero = jnp.zeros_like(f[0])
    even_f = jnp.where(pore, 0.5 - 0.5 * flow_plus, jnp.where(solid, 0.5, 0.0))
    odd_f = jnp.where(pore, 0.5 - 0.5 * flow_minus, jnp.where(solid, -0.5, 0.0))
    even_g = jnp.where(pore, 0.5 - 0.5 * solute_plus, jnp.where(solid, 0.5, 0.0))
    odd_g = jnp.where(pore, 0.5 - 0.5 * solute_minus, jnp.where(solid, -0.5, 0.0))
    level_f = jnp.where(inlet, inlet_density, jnp.where(solid, 0.0, outlet_density))
    level_g = jnp.where(inlet, inlet_solute, 0.0)

    total = {i: f[i] + f[i + 1] for i in range(1, 19, 2)}
    differ = {i: f[i] - f[i + 1] for i in range(1, 19, 2)}
    density = f[0]
    for i in range(1, 19, 2):
        density = density + total[i]
    mom = []
    for axis in range(3):
        summed = None
        for i in range(1, 19, 2):
            c = flow_velocity[i][axis]
            if c:
                term = differ[i]
                summed = term if summed is None else (summed + term if c > 0 else summed - term)
        mom.append(jnp.where(pore, summed, zero))
    square = mom[0] * mom[0] + mom[1] * mom[1] + mom[2] * mom[2]
    rest = jnp.where(pore, flow_plus * density - (flow_plus * 1.5) * square, level_f)

    out = [None] * 26
    weighted = {}
    for w in (1.0 / 3.0, 1.0 / 18.0, 1.0 / 36.0):
        weighted[w] = rest * w
    out[0] = (even_f + even_f) * f[0] + weighted[flow_weight[0]]
    projections = {}
    for i in range(1, 19, 2):
        w = flow_weight[i]
        projection = None
        for axis in range(3):
            c = flow_velocity[i][axis]
            if c:
                if projection is None:
                    projection = mom[axis]
                else:
                    projection = projection + mom[axis] if c > 0 else projection - mom[axis]
        projections[i] = projection
        even = even_f * total[i] + weighted[w] + (flow_plus * 4.5 * w) * (projection * projection)
        odd = odd_f * differ[i] + (flow_minus * 3.0 * w) * projection
        out[i] = even + odd
        out[i + 1] = even - odd

    g = f[19:]
    total_g = {k: g[k] + g[k + 1] for k in (1, 3, 5)}
    conc = g[0] + total_g[1] + total_g[3] + total_g[5]
    drift = (solute_minus * 4.0 * 0.125) * conc
    rest_g = jnp.where(pore, solute_plus * conc, level_g)
    out[19] = (even_g + even_g) * g[0] + 0.25 * rest_g
    share = 0.125 * rest_g
    for k in (1, 3, 5):
        even = even_g * total_g[k] + share
        odd = odd_g * (g[k] - g[k + 1]) + drift * projections[k]
        out[19 + k] = even + odd
        out[20 + k] = even - odd
    return out


def kernel(
    flow, solute, kind, density, momentum, conc,
    fin, kin, w0, wp, wm,
    in_sem, ys_sem, yr_sem, xs_sem, xr_sem, cs_sem, cr_sem,
):
    half = fin.shape[1] // 2
    per = half // CHUNKS
    last = CHUNKS - 1
    nx = lax.axis_size("gx")
    ny = lax.axis_size("gy")
    ix = lax.axis_index("gx")
    iy = lax.axis_index("gy")
    xs = {-1: lax.rem(ix + nx - 1, nx), 0: ix, 1: lax.rem(ix + 1, nx)}
    ys = {-1: lax.rem(iy + ny - 1, ny), 0: iy, 1: lax.rem(iy + 1, ny)}

    def device(dx, dy):
        return {"gx": xs[dx], "gy": ys[dy]}

    def remote(src, dst, send, recv, dx, dy):
        return pltpu.make_async_remote_copy(
            src_ref=src, dst_ref=dst, send_sem=send, recv_sem=recv,
            device_id=device(dx, dy), device_id_type=pl.DeviceIdType.MESH,
        )

    def y_copy(s, b, up):
        cols = pl.ds(2 * per * b, 2 * per)
        if up:
            src, dst = wp.at[s, :, cols, 15:16, :], wp.at[s, :, cols, 7:8, :]
        else:
            src, dst = wm.at[s, :, cols, 0:1, :], wm.at[s, :, cols, 8:9, :]
        k = 0 if up else 1
        return remote(src, dst, ys_sem.at[s, k, b], yr_sem.at[s, k, b], 0, 1 if up else -1)

    def x_copies(s, right):
        k = 0 if right else 1
        here, there = (2 * half - 1, 2 * half) if right else (2 * half - 2, 2 * half + 1)
        dx = 1 if right else -1
        parts = [
            (w0, pl.ds(4 * k, 4), pl.ds(0, 8)),
            (wp, pl.ds(k, 1), pl.ds(8, 8)),
            (wm, pl.ds(k, 1), pl.ds(0, 8)),
        ]
        return [
            remote(
                ref.at[s, pops, here, rows, :], ref.at[s, pops, there, rows, :],
                xs_sem.at[s, k, n], xr_sem.at[s, k, n], dx, 0,
            )
            for n, (ref, pops, rows) in enumerate(parts)
        ]

    def corner_copies(s, right):
        k = 0 if right else 1
        here, there = (2 * half - 1, 2 * half) if right else (2 * half - 2, 2 * half + 1)
        dx = 1 if right else -1
        up = remote(
            wp.at[s, k, here, 15:16, :], wp.at[s, k, there, 7:8, :],
            cs_sem.at[s, k, 0], cr_sem.at[s, k, 0], dx, 1,
        )
        down = remote(
            wm.at[s, k, here, 0:1, :], wm.at[s, k, there, 8:9, :],
            cs_sem.at[s, k, 1], cr_sem.at[s, k, 1], dx, -1,
        )
        return [up, down]

    def load_copies(b):
        copies = []
        for side, start in enumerate((half - per * (b + 1), half + per * b)):
            cols = pl.ds(start, per)
            copies += [
                pltpu.make_async_copy(flow.at[:, cols], fin.at[0:19, cols], in_sem.at[b, side, 0]),
                pltpu.make_async_copy(solute.at[:, cols], fin.at[19:26, cols], in_sem.at[b, side, 1]),
                pltpu.make_async_copy(kind.at[cols], kin.at[cols], in_sem.at[b, side, 2]),
            ]
        return copies

    barrier = pltpu.get_barrier_semaphore()
    for dx in (-1, 0, 1):
        for dy in (-1, 0, 1):
            if dx or dy:
                pl.semaphore_signal(
                    barrier, inc=1, device_id=device(dx, dy), device_id_type=pl.DeviceIdType.MESH
                )
    for c in range(CHUNKS):
        for copy in load_copies(c):
            copy.start()

    lane = lax.broadcasted_iota(jnp.int32, (8, 128), 1)
    depth = 128

    def shifted(value, along_z):
        if along_z == 1:
            return jnp.where(lane == 0, 0.0, pltpu.roll(value, 1, axis=1))
        if along_z == -1:
            return jnp.where(lane == depth - 1, 0.0, pltpu.roll(value, depth - 1, axis=1))
        return value

    def places(c):
        found = []
        for n in range(per):
            j = per * c + n
            found.append((half - 1 - j, 2 * j, {
                1: 2 * j + 2, 0: 2 * j, -1: jnp.where(j == 0, 1, 2 * j - 2),
            }))
            found.append((half + j, 2 * j + 1, {
                1: jnp.maximum(2 * j - 1, 0), 0: 2 * j + 1, -1: 2 * j + 3,
            }))
        return found

    def pull(s, source):
        f = [None] * 26
        for group, ref, rows in (
            (still, w0, slice(0, 8)), (upward, wp, slice(7, 15)), (downward, wm, slice(1, 9)),
        ):
            for n, p in enumerate(group):
                f[p] = ref[s, n, source[all_velocity[p][0]], rows, :]
        return f

    def push(s, place, out):
        for group, ref, rows in (
            (still, w0, slice(0, 8)), (upward, wp, slice(8, 16)), (downward, wm, slice(0, 8)),
        ):
            for n, p in enumerate(group):
                ref[s, n, place, rows, :] = shifted(out[p], all_velocity[p][2])

    def arrive(s, c):
        @pl.when(c == 0)
        def _():
            y_copy(s, 0, True).wait_recv()
            y_copy(s, 0, False).wait_recv()

        @pl.when(c < last)
        def _():
            y_copy(s, c + 1, True).wait_recv()
            y_copy(s, c + 1, False).wait_recv()

        @pl.when(c == last)
        def _():
            for right in (True, False):
                for copy in x_copies(s, right) + corner_copies(s, right):
                    copy.wait_recv()

    def depart(s, c):
        @pl.when(c == last)
        def _():
            for right in (True, False):
                for copy in corner_copies(s, right):
                    copy.start()

        y_copy(s, c, True).start()
        y_copy(s, c, False).start()

        @pl.when(c == last)
        def _():
            for right in (True, False):
                for copy in x_copies(s, right):
                    copy.start()

    for s in range(STEPS):
        def stage(c, carry):
            if s == 0:
                for copy in load_copies(c):
                    copy.wait()
            else:
                arrive(s - 1, c)
            for x, place, source in places(c):
                f = [fin[p, x] for p in range(26)] if s == 0 else pull(s - 1, source)
                push(s, place, collide(f, kin[x]))
            if s == 0:
                @pl.when(c == 0)
                def _():
                    pl.semaphore_wait(barrier, 8)
            depart(s, c)
            return carry

        lax.fori_loop(0, CHUNKS, stage, 0)

    def finish(c, carry):
        arrive(STEPS - 1, c)
        for x, _, source in places(c):
            f = pull(STEPS - 1, source)
            summed = f[0]
            for i in range(1, 19):
                summed = summed + f[i]
            density[x] = summed
            for axis in range(3):
                summed = None
                for i in range(1, 19):
                    v = flow_velocity[i][axis]
                    if v:
                        summed = f[i] if summed is None else (summed + f[i] if v > 0 else summed - f[i])
                momentum[axis, x] = summed
            summed = f[19]
            for i in range(20, 26):
                summed = summed + f[i]
            conc[x] = summed
        return carry

    lax.fori_loop(0, CHUNKS, finish, 0)

    for s in range(STEPS):
        for b in range(CHUNKS):
            y_copy(s, b, True).wait_send()
            y_copy(s, b, False).wait_send()
        for right in (True, False):
            for copy in x_copies(s, right) + corner_copies(s, right):
                copy.wait_send()


def local(flow_populations, solute_populations, voxel_kind):
    cells_x, cells_y, depth = voxel_kind.shape
    f32 = jnp.float32
    block = (cells_x, cells_y, depth)
    return pl.pallas_call(
        kernel,
        out_shape=(
            jax.ShapeDtypeStruct(block, f32),
            jax.ShapeDtypeStruct((3, *block), f32),
            jax.ShapeDtypeStruct(block, f32),
        ),
        in_specs=[pl.BlockSpec(memory_space=pl.ANY)] * 3,
        out_specs=[pl.BlockSpec(memory_space=pltpu.VMEM)] * 3,
        scratch_shapes=[
            pltpu.VMEM((26, *block), f32),
            pltpu.VMEM(block, jnp.int32),
            pltpu.VMEM((STEPS, 14, cells_x + 2, 8, depth), f32),
            pltpu.VMEM((STEPS, 6, cells_x + 2, 16, depth), f32),
            pltpu.VMEM((STEPS, 6, cells_x + 2, 16, depth), f32),
            pltpu.SemaphoreType.DMA((CHUNKS, 2, 3)),
            pltpu.SemaphoreType.DMA((STEPS, 2, CHUNKS)),
            pltpu.SemaphoreType.DMA((STEPS, 2, CHUNKS)),
            pltpu.SemaphoreType.DMA((STEPS, 2, 3)),
            pltpu.SemaphoreType.DMA((STEPS, 2, 3)),
            pltpu.SemaphoreType.DMA((STEPS, 2, 2)),
            pltpu.SemaphoreType.DMA((STEPS, 2, 2)),
        ],
        compiler_params=pltpu.CompilerParams(
            collective_id=0, has_side_effects=True, vmem_limit_bytes=24 * 1024 * 1024
        ),
        name="lattice",
    )(*(pltpu.with_memory_space_constraint(a, pltpu.HBM) for a in (flow_populations, solute_populations, voxel_kind)))


def solution(mesh):
    placed = (P(None, "gx", "gy", None), P(None, "gx", "gy", None), P("gx", "gy", None))
    return jax.shard_map(
        local,
        mesh=mesh,
        in_specs=placed,
        out_specs=(P("gx", "gy", None), P(None, "gx", "gy", None), P("gx", "gy", None)),
        check_vma=False,
    )
```

time: 92 us -> 41 us (0.45)
  the two profiles are of different devices: /device:TPU:8 before, /device:TPU:1 now
where the time goes in v1:
time: 41 us; the launch traced here: 40.9 us
  Pallas kernels  38.3 us (93%)
  local copies, waits for them, and re-layouts  1.94 us (5%)
  between operations  0.64 us (2%)
    pallas_call x1, Pallas kernels, local(): pl.pallas_call(kernel, out_shape=(jax.ShapeDtypeStruct(block, f32), jax.S...  38.3 us
    unnamed x3, local copies, waits for them, and re-layouts  1.94 us

profile of v1, /device:TPU:1, one launch (start us, length us, event | category | flops | bytes accessed | tf_op | source)
XLA Modules:
  0.0 40.9 jit_solution(4872275311403563218)
XLA Ops:
  0.6 38.3 %lattice.1 = (f32[16,8,128]{2,1,0:T(8,128)S(1)}, f32[3,16,8,128]{3,2,1,0:T(8,128)S(1)}, f32[16,8,128]{2,1,0:T(8,128)S(1)}) custom-call(f32[19,16,8,128]{3,2,1,0:T(8,128)} %flow.1, f32[7,16,8,128]{3,2,1,0:T(8,128)} %solute.1, s32[16,8,128]{2,1,0:T(8,128)} %kind.1), custom_call_target="tpu_custom_call" | custom-call | tf_op jit(solution)/shard_map/lattice/pallas_call | solution.py:326
  38.9 0.6 %copy.9 = f32[16,8,128]{2,1,0:T(8,128)} copy(f32[16,8,128]{2,1,0:T(8,128)S(1)} %get-tuple-element.6) | data formatting | bytes 131072
  39.5 0.7 %copy.10 = f32[3,16,8,128]{3,2,1,0:T(8,128)} copy(f32[3,16,8,128]{3,2,1,0:T(8,128)S(1)} %get-tuple-element.7) | data formatting | bytes 393216
  40.2 0.6 %copy.11 = f32[16,8,128]{2,1,0:T(8,128)} copy(f32[16,8,128]{2,1,0:T(8,128)S(1)} %get-tuple-element.8) | data formatting | bytes 131072

commit v2 on v1

--- a/solution.py
+++ b/solution.py
@@ -45,17 +45,23 @@
 downward = [9, 8, 4, 16, 18, 23]
 
 
-def collide(f, kind):
+def coefficients(kind):
     pore = kind == 0
     solid = kind == 1
     inlet = kind == 2
-    zero = jnp.zeros_like(f[0])
     even_f = jnp.where(pore, 0.5 - 0.5 * flow_plus, jnp.where(solid, 0.5, 0.0))
     odd_f = jnp.where(pore, 0.5 - 0.5 * flow_minus, jnp.where(solid, -0.5, 0.0))
     even_g = jnp.where(pore, 0.5 - 0.5 * solute_plus, jnp.where(solid, 0.5, 0.0))
     odd_g = jnp.where(pore, 0.5 - 0.5 * solute_minus, jnp.where(solid, -0.5, 0.0))
     level_f = jnp.where(inlet, inlet_density, jnp.where(solid, 0.0, outlet_density))
     level_g = jnp.where(inlet, inlet_solute, 0.0)
+    return even_f, odd_f, even_g, odd_g, level_f, level_g
+
+
+def collide(f, kind, factors):
+    pore = kind == 0
+    zero = jnp.zeros_like(f[0])
+    even_f, odd_f, even_g, odd_g, level_f, level_g = factors
 
     total = {i: f[i] + f[i + 1] for i in range(1, 19, 2)}
     differ = {i: f[i] - f[i + 1] for i in range(1, 19, 2)}
@@ -113,7 +119,7 @@
 
 def kernel(
     flow, solute, kind, density, momentum, conc,
-    fin, kin, w0, wp, wm,
+    fin, kin, fac, w0, wp, wm,
     in_sem, ys_sem, yr_sem, xs_sem, xr_sem, cs_sem, cr_sem,
 ):
     half = fin.shape[1] // 2
@@ -193,7 +199,7 @@
                 pl.semaphore_signal(
                     barrier, inc=1, device_id=device(dx, dy), device_id_type=pl.DeviceIdType.MESH
                 )
-    for c in range(CHUNKS):
+    for c in reversed(range(CHUNKS)):
         for copy in load_copies(c):
             copy.start()
 
@@ -207,17 +213,11 @@
             return jnp.where(lane == depth - 1, 0.0, pltpu.roll(value, depth - 1, axis=1))
         return value
 
-    def places(c):
-        found = []
-        for n in range(per):
-            j = per * c + n
-            found.append((half - 1 - j, 2 * j, {
-                1: 2 * j + 2, 0: 2 * j, -1: jnp.where(j == 0, 1, 2 * j - 2),
-            }))
-            found.append((half + j, 2 * j + 1, {
-                1: jnp.maximum(2 * j - 1, 0), 0: 2 * j + 1, -1: 2 * j + 3,
-            }))
-        return found
+    def places(j):
+        return [
+            (half - 1 - j, 2 * j, {1: 2 * j + 2, 0: 2 * j, -1: 2 * j - 2 if j else 1}),
+            (half + j, 2 * j + 1, {1: 2 * j - 1 if j else 0, 0: 2 * j + 1, -1: 2 * j + 3}),
+        ]
 
     def pull(s, source):
         f = [None] * 26
@@ -235,80 +235,70 @@
             for n, p in enumerate(group):
                 ref[s, n, place, rows, :] = shifted(out[p], all_velocity[p][2])
 
-    def arrive(s, c):
-        @pl.when(c == 0)
-        def _():
-            y_copy(s, 0, True).wait_recv()
-            y_copy(s, 0, False).wait_recv()
-
-        @pl.when(c < last)
-        def _():
-            y_copy(s, c + 1, True).wait_recv()
-            y_copy(s, c + 1, False).wait_recv()
-
-        @pl.when(c == last)
-        def _():
-            for right in (True, False):
-                for copy in x_copies(s, right) + corner_copies(s, right):
-                    copy.wait_recv()
-
-    def depart(s, c):
-        @pl.when(c == last)
-        def _():
-            for right in (True, False):
-                for copy in corner_copies(s, right):
-                    copy.start()
-
-        y_copy(s, c, True).start()
-        y_copy(s, c, False).start()
-
-        @pl.when(c == last)
-        def _():
-            for right in (True, False):
-                for copy in x_copies(s, right):
-                    copy.start()
+    def y_arrive(s, c):
+        for b in (last, last - 1) if c == last else ((c - 1,) if c else ()):
+            y_copy(s, b, True).wait_recv()
+            y_copy(s, b, False).wait_recv()
+
+    def x_arrive(s):
+        for right in (True, False):
+            for copy in x_copies(s, right) + corner_copies(s, right):
+                copy.wait_recv()
+
+    def start(copies):
+        for copy in copies:
+            copy.start()
 
     for s in range(STEPS):
-        def stage(c, carry):
+        for c in reversed(range(CHUNKS)):
             if s == 0:
                 for copy in load_copies(c):
                     copy.wait()
             else:
-                arrive(s - 1, c)
-            for x, place, source in places(c):
-                f = [fin[p, x] for p in range(26)] if s == 0 else pull(s - 1, source)
-                push(s, place, collide(f, kin[x]))
-            if s == 0:
-                @pl.when(c == 0)
-                def _():
-                    pl.semaphore_wait(barrier, 8)
-            depart(s, c)
-            return carry
-
-        lax.fori_loop(0, CHUNKS, stage, 0)
-
-    def finish(c, carry):
-        arrive(STEPS - 1, c)
-        for x, _, source in places(c):
-            f = pull(STEPS - 1, source)
-            summed = f[0]
-            for i in range(1, 19):
-                summed = summed + f[i]
-            density[x] = summed
-            for axis in range(3):
-                summed = None
+                y_arrive(s - 1, c)
+            for j in range(per * c, per * (c + 1)):
+                if s and j == half - 1:
+                    x_arrive(s - 1)
+                for x, place, source in places(j):
+                    if s:
+                        f = pull(s - 1, source)
+                        factors = [fac[n, x] for n in range(6)]
+                    else:
+                        f = [fin[p, x] for p in range(26)]
+                        factors = coefficients(kin[x])
+                        for n in range(6):
+                            fac[n, x] = factors[n]
+                    push(s, place, collide(f, kin[x], factors))
+            if s == 0 and c == last:
+                pl.semaphore_wait(barrier, 8)
+            if c == last:
+                start(corner_copies(s, True) + corner_copies(s, False))
+            start([y_copy(s, c, True), y_copy(s, c, False)])
+            if c == last:
+                start(x_copies(s, True) + x_copies(s, False))
+
+    for c in reversed(range(CHUNKS)):
+        y_arrive(STEPS - 1, c)
+        for j in range(per * c, per * (c + 1)):
+            if j == half - 1:
+                x_arrive(STEPS - 1)
+            for x, _, source in places(j):
+                f = pull(STEPS - 1, source)
+                summed = f[0]
                 for i in range(1, 19):
-                    v = flow_velocity[i][axis]
-                    if v:
-                        summed = f[i] if summed is None else (summed + f[i] if v > 0 else summed - f[i])
-                momentum[axis, x] = summed
-            summed = f[19]
-            for i in range(20, 26):
-                summed = summed + f[i]
-            conc[x] = summed
-        return carry
-
-    lax.fori_loop(0, CHUNKS, finish, 0)
+                    summed = summed + f[i]
+                density[x] = summed
+                for axis in range(3):
+                    summed = None
+                    for i in range(1, 19):
+                        v = flow_velocity[i][axis]
+                        if v:
+                            summed = f[i] if summed is None else (summed + f[i] if v > 0 else summed - f[i])
+                    momentum[axis, x] = summed
+                summed = f[19]
+                for i in range(20, 26):
+                    summed = summed + f[i]
+                conc[x] = summed
 
     for s in range(STEPS):
         for b in range(CHUNKS):
@@ -319,11 +309,24 @@
                 copy.wait_send()
 
 
+def hand_over(density, momentum, conc, density_out, momentum_out, conc_out, sem):
+    copies = [
+        pltpu.make_async_copy(src, dst, sem.at[n])
+        for n, (src, dst) in enumerate(
+            ((momentum, momentum_out), (density, density_out), (conc, conc_out))
+        )
+    ]
+    for copy in copies:
+        copy.start()
+    for copy in copies:
+        copy.wait()
+
+
 def local(flow_populations, solute_populations, voxel_kind):
     cells_x, cells_y, depth = voxel_kind.shape
     f32 = jnp.float32
     block = (cells_x, cells_y, depth)
-    return pl.pallas_call(
+    results = pl.pallas_call(
         kernel,
         out_shape=(
             jax.ShapeDtypeStruct(block, f32),
@@ -335,6 +338,7 @@
         scratch_shapes=[
             pltpu.VMEM((26, *block), f32),
             pltpu.VMEM(block, jnp.int32),
+            pltpu.VMEM((6, *block), f32),
             pltpu.VMEM((STEPS, 14, cells_x + 2, 8, depth), f32),
             pltpu.VMEM((STEPS, 6, cells_x + 2, 16, depth), f32),
             pltpu.VMEM((STEPS, 6, cells_x + 2, 16, depth), f32),
@@ -351,6 +355,15 @@
         ),
         name="lattice",
     )(*(pltpu.with_memory_space_constraint(a, pltpu.HBM) for a in (flow_populations, solute_populations, voxel_kind)))
+    return pl.pallas_call(
+        hand_over,
+        out_shape=[jax.ShapeDtypeStruct(r.shape, f32) for r in results],
+        in_specs=[pl.BlockSpec(memory_space=pltpu.VMEM)] * 3,
+        out_specs=[pl.BlockSpec(memory_space=pltpu.HBM)] * 3,
+        scratch_shapes=[pltpu.SemaphoreType.DMA((3,))],
+        compiler_params=pltpu.CompilerParams(vmem_limit_bytes=4 * 1024 * 1024),
+        name="hand_over",
+    )(*results)
 
 
 def solution(mesh):

time: 41 us -> 38.1 us (0.929)
  local copies, waits for them, and re-layouts: 1.94 us -> 0 us
  Pallas kernels: 38.3 us -> 37.3 us
    unnamed x3 -> x0, local copies, waits for them, and re-layouts: 1.94 us -> none
    pallas_call x1, Pallas kernels: 38.3 us -> 36.6 us  [local(): pl.pallas_call(kernel, out_shape=(jax.ShapeDtypeStruct(block, f32), jax.S...]
    pallas_call x0 -> x1, Pallas kernels: none -> 0.74 us  [local(): pl.pallas_call(hand_over, out_shape=[jax.ShapeDtypeStruct(r.shape, f32) f...]
where the time goes in v2:
time: 38.1 us; the launch traced here: 38 us
  Pallas kernels  37.3 us (98%)
  between operations  0.64 us (2%)
    pallas_call x1, Pallas kernels, local(): pl.pallas_call(kernel, out_shape=(jax.ShapeDtypeStruct(block, f32), jax.S...  36.6 us

profile of v2, /device:TPU:1, one launch (start us, length us, event | category | flops | bytes accessed | tf_op | source)
XLA Modules:
  0.0 38.0 jit_solution(7853931382254658008)
XLA Ops:
  0.6 36.6 %lattice.1 = (f32[16,8,128]{2,1,0:T(8,128)S(1)}, f32[3,16,8,128]{3,2,1,0:T(8,128)S(1)}, f32[16,8,128]{2,1,0:T(8,128)S(1)}) custom-call(f32[19,16,8,128]{3,2,1,0:T(8,128)} %flow.1, f32[7,16,8,128]{3,2,1,0:T(8,128)} %solute.1, s32[16,8,128]{2,1,0:T(8,128)} %kind.1), custom_call_target="tpu_custom_call" | custom-call | tf_op jit(solution)/shard_map/lattice/pallas_call | solution.py:329
  37.2 0.7 %hand_over.1 = (f32[16,8,128]{2,1,0:T(8,128)}, f32[3,16,8,128]{3,2,1,0:T(8,128)}, f32[16,8,128]{2,1,0:T(8,128)}) custom-call(f32[16,8,128]{2,1,0:T(8,128)S(1)} %get-tuple-element.6.density, f32[3,16,8,128]{3,2,1,0:T(8,128)S(1)} %get-tuple-element.7.momentum, f32[16,8,128]{2,1,0:T(8,128)S(1)} %get-tuple-element.8.conc), custom_call_target="tpu_custom_call" | custom-call | tf_op jit(solution)/shard_map/hand_over/pallas_call | solution.py:358

commit v3 on v2

--- a/solution.py
+++ b/solution.py
@@ -120,7 +120,7 @@
 def kernel(
     flow, solute, kind, density, momentum, conc,
     fin, kin, fac, w0, wp, wm,
-    in_sem, ys_sem, yr_sem, xs_sem, xr_sem, cs_sem, cr_sem,
+    in_sem, y_sem, x_sem, send_sem,
 ):
     half = fin.shape[1] // 2
     per = half // CHUNKS
@@ -147,8 +147,7 @@
             src, dst = wp.at[s, :, cols, 15:16, :], wp.at[s, :, cols, 7:8, :]
         else:
             src, dst = wm.at[s, :, cols, 0:1, :], wm.at[s, :, cols, 8:9, :]
-        k = 0 if up else 1
-        return remote(src, dst, ys_sem.at[s, k, b], yr_sem.at[s, k, b], 0, 1 if up else -1)
+        return remote(src, dst, send_sem.at[0], y_sem.at[s, b], 0, 1 if up else -1)
 
     def x_copies(s, right):
         k = 0 if right else 1
@@ -162,9 +161,9 @@
         return [
             remote(
                 ref.at[s, pops, here, rows, :], ref.at[s, pops, there, rows, :],
-                xs_sem.at[s, k, n], xr_sem.at[s, k, n], dx, 0,
+                send_sem.at[0], x_sem.at[s], dx, 0,
             )
-            for n, (ref, pops, rows) in enumerate(parts)
+            for ref, pops, rows in parts
         ]
 
     def corner_copies(s, right):
@@ -173,25 +172,46 @@
         dx = 1 if right else -1
         up = remote(
             wp.at[s, k, here, 15:16, :], wp.at[s, k, there, 7:8, :],
-            cs_sem.at[s, k, 0], cr_sem.at[s, k, 0], dx, 1,
+            send_sem.at[1], x_sem.at[s], dx, 1,
         )
         down = remote(
             wm.at[s, k, here, 0:1, :], wm.at[s, k, there, 8:9, :],
-            cs_sem.at[s, k, 1], cr_sem.at[s, k, 1], dx, -1,
+            send_sem.at[1], x_sem.at[s], dx, -1,
         )
         return [up, down]
 
     def load_copies(b):
         copies = []
-        for side, start in enumerate((half - per * (b + 1), half + per * b)):
+        for start in (half - per * (b + 1), half + per * b):
             cols = pl.ds(start, per)
             copies += [
-                pltpu.make_async_copy(flow.at[:, cols], fin.at[0:19, cols], in_sem.at[b, side, 0]),
-                pltpu.make_async_copy(solute.at[:, cols], fin.at[19:26, cols], in_sem.at[b, side, 1]),
-                pltpu.make_async_copy(kind.at[cols], kin.at[cols], in_sem.at[b, side, 2]),
+                pltpu.make_async_copy(flow.at[:, cols], fin.at[0:19, cols], in_sem.at[b]),
+                pltpu.make_async_copy(solute.at[:, cols], fin.at[19:26, cols], in_sem.at[b]),
+                pltpu.make_async_copy(kind.at[cols], kin.at[cols], in_sem.at[b]),
             ]
         return copies
 
+    def loaded(b):
+        rows = fin.at[0:9, 0 : 6 * per]
+        pltpu.make_async_copy(rows, rows, in_sem.at[b]).wait()
+
+    def y_landed(s, b):
+        rows = wp.at[s, :, pl.ds(2 * per * b, 2 * per), 7:9, :]
+        remote(rows, rows, send_sem.at[0], y_sem.at[s, b], 0, 1).wait_recv()
+
+    def x_landed(s):
+        rows = wp.at[s, 0:5, 0:10, 0:2, :]
+        remote(rows, rows, send_sem.at[0], x_sem.at[s], 1, 0).wait_recv()
+
+    def all_sent():
+        rows = fin.at[0:9, 0 : 4 * STEPS]
+        remote(rows, rows, send_sem.at[0], x_sem.at[0], 1, 0).wait_send()
+        rows = wp.at[0, 0 : 2 * STEPS, 0:2, 0:1, :]
+        remote(rows, rows, send_sem.at[1], x_sem.at[0], 1, 0).wait_send()
+
+    for c in reversed(range(CHUNKS)):
+        for copy in load_copies(c):
+            copy.start()
     barrier = pltpu.get_barrier_semaphore()
     for dx in (-1, 0, 1):
         for dy in (-1, 0, 1):
@@ -199,9 +219,6 @@
                 pl.semaphore_signal(
                     barrier, inc=1, device_id=device(dx, dy), device_id_type=pl.DeviceIdType.MESH
                 )
-    for c in reversed(range(CHUNKS)):
-        for copy in load_copies(c):
-            copy.start()
 
     lane = lax.broadcasted_iota(jnp.int32, (8, 128), 1)
     depth = 128
@@ -237,13 +254,7 @@
 
     def y_arrive(s, c):
         for b in (last, last - 1) if c == last else ((c - 1,) if c else ()):
-            y_copy(s, b, True).wait_recv()
-            y_copy(s, b, False).wait_recv()
-
-    def x_arrive(s):
-        for right in (True, False):
-            for copy in x_copies(s, right) + corner_copies(s, right):
-                copy.wait_recv()
+            y_landed(s, b)
 
     def start(copies):
         for copy in copies:
@@ -252,13 +263,16 @@
     for s in range(STEPS):
         for c in reversed(range(CHUNKS)):
             if s == 0:
-                for copy in load_copies(c):
-                    copy.wait()
+                loaded(c)
             else:
                 y_arrive(s - 1, c)
-            for j in range(per * c, per * (c + 1)):
-                if s and j == half - 1:
-                    x_arrive(s - 1)
+            order = list(range(per * c, per * (c + 1)))
+            if s == 0 and c == last:
+                order.reverse()
+            for j in order:
+                edge = j == half - 1
+                if s and edge:
+                    x_landed(s - 1)
                 for x, place, source in places(j):
                     if s:
                         f = pull(s - 1, source)
@@ -269,44 +283,42 @@
                         for n in range(6):
                             fac[n, x] = factors[n]
                     push(s, place, collide(f, kin[x], factors))
-            if s == 0 and c == last:
-                pl.semaphore_wait(barrier, 8)
-            if c == last:
-                start(corner_copies(s, True) + corner_copies(s, False))
+                if edge:
+                    if s == 0:
+                        pl.semaphore_wait(barrier, 8)
+                    start(corner_copies(s, True) + corner_copies(s, False))
             start([y_copy(s, c, True), y_copy(s, c, False)])
             if c == last:
                 start(x_copies(s, True) + x_copies(s, False))
 
+    def finish(x, source):
+        f = pull(STEPS - 1, source)
+        summed = f[0]
+        for i in range(1, 19):
+            summed = summed + f[i]
+        density[x] = summed
+        for axis in range(3):
+            summed = None
+            for i in range(1, 19):
+                v = flow_velocity[i][axis]
+                if v:
+                    summed = f[i] if summed is None else (summed + f[i] if v > 0 else summed - f[i])
+            momentum[axis, x] = summed
+        summed = f[19]
+        for i in range(20, 26):
+            summed = summed + f[i]
+        conc[x] = summed
+
     for c in reversed(range(CHUNKS)):
         y_arrive(STEPS - 1, c)
         for j in range(per * c, per * (c + 1)):
-            if j == half - 1:
-                x_arrive(STEPS - 1)
-            for x, _, source in places(j):
-                f = pull(STEPS - 1, source)
-                summed = f[0]
-                for i in range(1, 19):
-                    summed = summed + f[i]
-                density[x] = summed
-                for axis in range(3):
-                    summed = None
-                    for i in range(1, 19):
-                        v = flow_velocity[i][axis]
-                        if v:
-                            summed = f[i] if summed is None else (summed + f[i] if v > 0 else summed - f[i])
-                    momentum[axis, x] = summed
-                summed = f[19]
-                for i in range(20, 26):
-                    summed = summed + f[i]
-                conc[x] = summed
-
-    for s in range(STEPS):
-        for b in range(CHUNKS):
-            y_copy(s, b, True).wait_send()
-            y_copy(s, b, False).wait_send()
-        for right in (True, False):
-            for copy in x_copies(s, right) + corner_copies(s, right):
-                copy.wait_send()
+            if j < half - 1:
+                for x, _, source in places(j):
+                    finish(x, source)
+    x_landed(STEPS - 1)
+    for x, _, source in places(half - 1):
+        finish(x, source)
+    all_sent()
 
 
 def hand_over(density, momentum, conc, density_out, momentum_out, conc_out, sem):
@@ -342,13 +354,10 @@
             pltpu.VMEM((STEPS, 14, cells_x + 2, 8, depth), f32),
             pltpu.VMEM((STEPS, 6, cells_x + 2, 16, depth), f32),
             pltpu.VMEM((STEPS, 6, cells_x + 2, 16, depth), f32),
-            pltpu.SemaphoreType.DMA((CHUNKS, 2, 3)),
-            pltpu.SemaphoreType.DMA((STEPS, 2, CHUNKS)),
-            pltpu.SemaphoreType.DMA((STEPS, 2, CHUNKS)),
-            pltpu.SemaphoreType.DMA((STEPS, 2, 3)),
-            pltpu.SemaphoreType.DMA((STEPS, 2, 3)),
-            pltpu.SemaphoreType.DMA((STEPS, 2, 2)),
-            pltpu.SemaphoreType.DMA((STEPS, 2, 2)),
+            pltpu.SemaphoreType.DMA((CHUNKS,)),
+            pltpu.SemaphoreType.DMA((STEPS, CHUNKS)),
+            pltpu.SemaphoreType.DMA((STEPS,)),
+            pltpu.SemaphoreType.DMA((2,)),
         ],
         compiler_params=pltpu.CompilerParams(
             collective_id=0, has_side_effects=True, vmem_limit_bytes=24 * 1024 * 1024

time: 38.1 us -> 37 us (0.971)
  Pallas kernels: 37.3 us -> 36.2 us
    pallas_call x1, Pallas kernels: 36.6 us -> 35.4 us  [local(): pl.pallas_call(kernel, out_shape=(jax.ShapeDtypeStruct(block, f32), jax.S...]
where the time goes in v3:
time: 37 us; the launch traced here: 36.8 us
  Pallas kernels  36.2 us (98%)
  between operations  0.64 us (2%)
    pallas_call x1, Pallas kernels, local(): pl.pallas_call(kernel, out_shape=(jax.ShapeDtypeStruct(block, f32), jax.S...  35.4 us
    pallas_call x1, Pallas kernels, local(): pl.pallas_call(hand_over, out_shape=[jax.ShapeDtypeStruct(r.shape, f32) f...  0.74 us

profile of v3, /device:TPU:1, one launch (start us, length us, event | category | flops | bytes accessed | tf_op | source)
XLA Modules:
  0.0 36.8 jit_solution(8172897490139849755)
XLA Ops:
  0.6 35.4 %lattice.1 = (f32[16,8,128]{2,1,0:T(8,128)S(1)}, f32[3,16,8,128]{3,2,1,0:T(8,128)S(1)}, f32[16,8,128]{2,1,0:T(8,128)S(1)}) custom-call(f32[19,16,8,128]{3,2,1,0:T(8,128)} %flow.1, f32[7,16,8,128]{3,2,1,0:T(8,128)} %solute.1, s32[16,8,128]{2,1,0:T(8,128)} %kind.1), custom_call_target="tpu_custom_call" | custom-call | tf_op jit(solution)/shard_map/lattice/pallas_call | solution.py:341
  36.1 0.7 %hand_over.1 = (f32[16,8,128]{2,1,0:T(8,128)}, f32[3,16,8,128]{3,2,1,0:T(8,128)}, f32[16,8,128]{2,1,0:T(8,128)}) custom-call(f32[16,8,128]{2,1,0:T(8,128)S(1)} %get-tuple-element.6.density, f32[3,16,8,128]{3,2,1,0:T(8,128)S(1)} %get-tuple-element.7.momentum, f32[16,8,128]{2,1,0:T(8,128)S(1)} %get-tuple-element.8.conc), custom_call_target="tpu_custom_call" | custom-call | tf_op jit(solution)/shard_map/hand_over/pallas_call | solution.py:367

commit v4 on v3

--- a/solution.py
+++ b/solution.py
@@ -6,6 +6,7 @@
 from jax.sharding import PartitionSpec as P
 
 STEPS = 3
+GREETED = 3
 CHUNKS = 4
 
 flow_velocity = [
@@ -209,16 +210,14 @@
         rows = wp.at[0, 0 : 2 * STEPS, 0:2, 0:1, :]
         remote(rows, rows, send_sem.at[1], x_sem.at[0], 1, 0).wait_send()
 
+    barrier = pltpu.get_barrier_semaphore()
+    for dx, dy in ((1, 1), (1, -1), (-1, 1), (-1, -1), (0, 1), (0, -1), (1, 0), (-1, 0)):
+        pl.semaphore_signal(
+            barrier, inc=1, device_id=device(dx, dy), device_id_type=pl.DeviceIdType.MESH
+        )
     for c in reversed(range(CHUNKS)):
         for copy in load_copies(c):
             copy.start()
-    barrier = pltpu.get_barrier_semaphore()
-    for dx in (-1, 0, 1):
-        for dy in (-1, 0, 1):
-            if dx or dy:
-                pl.semaphore_signal(
-                    barrier, inc=1, device_id=device(dx, dy), device_id_type=pl.DeviceIdType.MESH
-                )
 
     lane = lax.broadcasted_iota(jnp.int32, (8, 128), 1)
     depth = 128
@@ -252,44 +251,56 @@
             for n, p in enumerate(group):
                 ref[s, n, place, rows, :] = shifted(out[p], all_velocity[p][2])
 
-    def y_arrive(s, c):
-        for b in (last, last - 1) if c == last else ((c - 1,) if c else ()):
-            y_landed(s, b)
-
     def start(copies):
         for copy in copies:
             copy.start()
 
+    def arrivals(s):
+        waited = set()
+
+        def wait(j):
+            for c in sorted({j // per, max(j - 1, 0) // per} - waited, reverse=True):
+                y_landed(s, c)
+                waited.add(c)
+
+        return wait
+
     for s in range(STEPS):
-        for c in reversed(range(CHUNKS)):
-            if s == 0:
+        arrive = arrivals(s - 1)
+        for j in reversed(range(half)):
+            c = j // per
+            edge = j == half - 1
+            if s:
+                arrive(j)
+                if edge:
+                    x_landed(s - 1)
+            elif (j + 1) % per == 0:
                 loaded(c)
-            else:
-                y_arrive(s - 1, c)
-            order = list(range(per * c, per * (c + 1)))
-            if s == 0 and c == last:
-                order.reverse()
-            for j in order:
-                edge = j == half - 1
-                if s and edge:
-                    x_landed(s - 1)
-                for x, place, source in places(j):
-                    if s:
-                        f = pull(s - 1, source)
-                        factors = [fac[n, x] for n in range(6)]
-                    else:
-                        f = [fin[p, x] for p in range(26)]
-                        factors = coefficients(kin[x])
-                        for n in range(6):
-                            fac[n, x] = factors[n]
-                    push(s, place, collide(f, kin[x], factors))
-                if edge:
-                    if s == 0:
-                        pl.semaphore_wait(barrier, 8)
-                    start(corner_copies(s, True) + corner_copies(s, False))
-            start([y_copy(s, c, True), y_copy(s, c, False)])
-            if c == last:
+            for x, place, source in places(j):
+                if s:
+                    f = pull(s - 1, source)
+                    factors = [fac[n, x] for n in range(6)]
+                else:
+                    f = [fin[p, x] for p in range(26)]
+                    factors = coefficients(kin[x])
+                    for n in range(6):
+                        fac[n, x] = factors[n]
+                push(s, place, collide(f, kin[x], factors))
+            if s == 0 and j > per * GREETED:
+                continue
+            if s == 0 and j == per * GREETED:
+                pl.semaphore_wait(barrier, 8)
+                start(corner_copies(s, True) + corner_copies(s, False))
+                for ready in reversed(range(GREETED, CHUNKS)):
+                    start([y_copy(s, ready, True), y_copy(s, ready, False)])
                 start(x_copies(s, True) + x_copies(s, False))
+                continue
+            if edge:
+                start(corner_copies(s, True) + corner_copies(s, False))
+            if j % per == 0:
+                start([y_copy(s, c, True), y_copy(s, c, False)])
+                if c == last:
+                    start(x_copies(s, True) + x_copies(s, False))
 
     def finish(x, source):
         f = pull(STEPS - 1, source)
@@ -309,12 +320,12 @@
             summed = summed + f[i]
         conc[x] = summed
 
-    for c in reversed(range(CHUNKS)):
-        y_arrive(STEPS - 1, c)
-        for j in range(per * c, per * (c + 1)):
-            if j < half - 1:
-                for x, _, source in places(j):
-                    finish(x, source)
+    arrive = arrivals(STEPS - 1)
+    for j in reversed(range(half - 1)):
+        arrive(j)
+        for x, _, source in places(j):
+            finish(x, source)
+    arrive(half - 1)
     x_landed(STEPS - 1)
     for x, _, source in places(half - 1):
         finish(x, source)

time: 37 us -> 36.9 us (level)
  no operation moved by 1% of the time
where the time goes in v4:
time: 36.9 us; the launch traced here: 36.7 us
  Pallas kernels  36.1 us (98%)
  between operations  0.64 us (2%)
    pallas_call x1, Pallas kernels, local(): pl.pallas_call(kernel, out_shape=(jax.ShapeDtypeStruct(block, f32), jax.S...  35.3 us
    pallas_call x1, Pallas kernels, local(): pl.pallas_call(hand_over, out_shape=[jax.ShapeDtypeStruct(r.shape, f32) f...  0.74 us

profile of v4, /device:TPU:1, one launch (start us, length us, event | category | flops | bytes accessed | tf_op | source)
XLA Modules:
  0.0 36.7 jit_solution(5049737241271479304)
XLA Ops:
  0.6 35.3 %lattice.1 = (f32[16,8,128]{2,1,0:T(8,128)S(1)}, f32[3,16,8,128]{3,2,1,0:T(8,128)S(1)}, f32[16,8,128]{2,1,0:T(8,128)S(1)}) custom-call(f32[19,16,8,128]{3,2,1,0:T(8,128)} %flow.1, f32[7,16,8,128]{3,2,1,0:T(8,128)} %solute.1, s32[16,8,128]{2,1,0:T(8,128)} %kind.1), custom_call_target="tpu_custom_call" | custom-call | tf_op jit(solution)/shard_map/lattice/pallas_call | solution.py:352
  36.0 0.7 %hand_over.1 = (f32[16,8,128]{2,1,0:T(8,128)}, f32[3,16,8,128]{3,2,1,0:T(8,128)}, f32[16,8,128]{2,1,0:T(8,128)}) custom-call(f32[16,8,128]{2,1,0:T(8,128)S(1)} %get-tuple-element.6.density, f32[3,16,8,128]{3,2,1,0:T(8,128)S(1)} %get-tuple-element.7.momentum, f32[16,8,128]{2,1,0:T(8,128)S(1)} %get-tuple-element.8.conc), custom_call_target="tpu_custom_call" | custom-call | tf_op jit(solution)/shard_map/hand_over/pallas_call | solution.py:378
